TPU v7x, 32 devices: a whole 2x2x4 slice. The times are simulated.
32 devices in a mesh: dp: 16 (over z, x, core), vol: 2 (over y).
Axes of the slice: x: 2, y: 2, z: 4, core: 2. Of those that a mesh axis runs over, the one named last changes fastest.
Arguments:
- images: float32 [32, 128, 128], P(('dp', 'vol')), may hold values from -6 to 6
- contrast: bfloat16 [32, 128, 128], P(('dp', 'vol')), may hold values from -1 to 1
- volume: bfloat16 [256, 256, 256], P('vol'), may hold values from -6 to 6
- line_index: int32 [32, 4, 128], P('dp'), may hold values from 0 to 65278, as said below
- patch_weight: bfloat16 [64, 1024], replicated, may hold values from -0.75 to 0.75
- position: bfloat16 [256, 1024], replicated, may hold values from -3 to 3
- norm_gain: float32 [1024], replicated, may hold values from 0.1 to 1.9
- project_in: bfloat16 [1024, 1536], P('dp'), may hold values from -0.1875 to 0.1875
- project_out: bfloat16 [1024, 512], P('dp'), may hold values from -0.25 to 0.25
- head_weight: float32 [1024, 4], replicated, may hold values from -1.8 to 1.8
Outputs:
- errors: float32 [32, 4], P(('dp', 'vol'))
- in_gradient: float32 [1024, 1536], P('dp')
- out_gradient: float32 [1024, 512], P('dp')
- head_gradient: float32 [1024, 4], replicated
Inputs may be any that keep to these rules, and one draw needn't show every extreme that they name: line_index[i, k, r] = z * 256 + y names the plane z and row y of the volume that row r of hypothesis k of image i samples; z and y lie within 0 and 254.
All inputs are finite; a program needn't handle non-finite values.
Results may differ from a plain program's by a relative error of at most 0.038.
Values may be sent and summed in bfloat16 or wider, within the bound.
A program may use at most 64 MiB of HBM per device.

v0:
```python
import math
import jax
import jax.numpy as jnp
from jax import lax
from jax.sharding import PartitionSpec as P

HEADS = 8
HEAD_DIM = 64
PIX = 128
PATCH = 8
PATCHES = 256
K = 4
EPSILON = 1e-05


def embed_images(images, patch_weight, position):
    count = images.shape[0]
    grid = PIX // PATCH
    pieces = images.reshape(count, grid, PATCH, grid, PATCH).transpose(0, 1, 3, 2, 4)
    pieces = pieces.reshape(count * grid * grid, PATCH * PATCH).astype(jnp.bfloat16)
    mixed = jnp.dot(pieces, patch_weight, preferred_element_type=jnp.float32)
    mixed = mixed.reshape(count, grid * grid, -1) + position.astype(jnp.float32)[None]
    return mixed.reshape(count * grid * grid, -1).astype(jnp.bfloat16)


def normalize(embedded, norm_gain):
    values = embedded.astype(jnp.float32)
    center = values - jnp.mean(values, axis=1, keepdims=True)
    scale = lax.rsqrt(jnp.mean(center * center, axis=1, keepdims=True) + EPSILON)
    return (center * scale * norm_gain[None, :]).astype(jnp.bfloat16)


def attend(triple):
    count = triple.shape[0] // PATCHES
    parts = triple.reshape(count, PATCHES, 3, HEADS, HEAD_DIM).astype(jnp.float32)
    query = parts[:, :, 0]
    keys = parts[:, :, 1]
    values = parts[:, :, 2]
    scores = jnp.einsum("bqhd,bkhd->bhqk", query, keys) * HEAD_DIM ** (-0.5)
    raised = jnp.exp(scores)
    weights = (raised / jnp.sum(raised, axis=-1, keepdims=True)).astype(jnp.bfloat16)
    mixed = jnp.einsum("bhqk,bkhd->bqhd", weights.astype(jnp.float32), values)
    return mixed.reshape(count * PATCHES, HEADS * HEAD_DIM).astype(jnp.bfloat16)


def hartley(images):
    side = images.shape[1]
    freq = jnp.arange(side, dtype=jnp.int32) - side // 2
    place = jnp.arange(side, dtype=jnp.int32)
    phase = (freq[:, None] * place[None, :] % side).astype(jnp.float32) * (2.0 * math.pi / side)
    cosine = jnp.cos(phase)
    sine = jnp.sin(phase)
    highest = lax.Precision.HIGHEST
    first_cos = jnp.einsum("rn,bnm->brm", cosine, images, precision=highest)
    first_sin = jnp.einsum("rn,bnm->brm", sine, images, precision=highest)
    result = jnp.einsum("brm,cm->brc", first_cos, cosine + sine, precision=highest)
    result = result + jnp.einsum("brm,cm->brc", first_sin, cosine - sine, precision=highest)
    return result / side


def render(volume, line_index, slab_index):
    slab, side, _ = volume.shape
    table = volume.reshape(slab * side, side)
    plane = line_index // side - slab_index * slab
    inside = (plane >= 0) & (plane < slab)
    rows = jnp.clip(plane, 0, slab - 1) * side + line_index % side
    picked = jnp.take(table, rows.reshape(-1), axis=0)[:, ::2]
    picked = jnp.where(inside.reshape(-1, 1), picked.astype(jnp.float32), 0.0)
    return (picked.reshape(line_index.shape[0], -1), inside)


def local(
    images,
    contrast,
    volume,
    line_index,
    patch_weight,
    position,
    norm_gain,
    project_in,
    project_out,
    head_weight,
):
    count = images.shape[0]
    width = norm_gain.shape[0]
    highest = lax.Precision.HIGHEST
    rendered, inside = render(volume, line_index, lax.axis_index("vol"))
    spectrum = hartley(images)
    slices = lax.psum_scatter(
        rendered.astype(jnp.bfloat16), "vol", scatter_dimension=0, tiled=True
    ).astype(jnp.float32)
    slices = slices.reshape(count, K, PIX, PIX)
    misfit = contrast.astype(jnp.float32)[:, None] * slices - spectrum[:, None]
    errors = jnp.mean(misfit * misfit, axis=(2, 3))
    embedded = embed_images(images, patch_weight, position)
    normed = normalize(embedded, norm_gain)
    triple = jnp.dot(
        normed,
        lax.all_gather(project_in, "dp", axis=0, tiled=True),
        preferred_element_type=jnp.float32,
    ).astype(jnp.bfloat16)
    attended = attend(triple)
    contract_last = (((1,), (1,)), ((), ()))
    out_whole = lax.all_gather(project_out, "dp", axis=0, tiled=True)
    branch = lax.dot_general(attended, out_whole, contract_last, preferred_element_type=jnp.float32)
    layer_out = embedded.astype(jnp.float32) + branch
    pooled = jnp.mean(layer_out.reshape(count, PATCHES, width), axis=1)
    logits = jnp.dot(pooled, head_weight, precision=highest)
    raised = jnp.exp(logits)
    chances = raised / jnp.sum(raised, axis=1, keepdims=True)
    expected = jnp.sum(chances * errors, axis=1, keepdims=True)
    logit_slope = chances * (errors - expected)
    head_gradient = lax.psum(jnp.dot(pooled.T, logit_slope, precision=highest), ("dp", "vol"))
    pooled_slope = jnp.dot(logit_slope, head_weight.T, precision=highest) / PATCHES
    layer_slope = jnp.broadcast_to(pooled_slope[:, None, :], (count, PATCHES, width))
    layer_slope = layer_slope.reshape(count * PATCHES, width).astype(jnp.bfloat16)
    attended_slope = jnp.dot(layer_slope, out_whole, preferred_element_type=jnp.float32).astype(
        jnp.bfloat16
    )
    triple_slope = jax.vjp(attend, triple)[1](attended_slope)[0]
    contract_first = (((0,), (0,)), ((), ()))
    first = lax.dot_general(
        normed, triple_slope, contract_first, preferred_element_type=jnp.float32
    )
    second = lax.dot_general(
        layer_slope, attended, contract_first, preferred_element_type=jnp.float32
    )
    shard = lax.psum_scatter(
        jnp.concatenate([first, second], axis=1).astype(jnp.bfloat16),
        "dp",
        scatter_dimension=0,
        tiled=True,
    ).astype(jnp.float32)
    shard = lax.psum(shard.astype(jnp.bfloat16), "vol").astype(jnp.float32)
    split = project_in.shape[1]
    return (errors, shard[:, :split], shard[:, split:], head_gradient)


def solution(mesh):
    placed = (
        P(("dp", "vol"), None, None),
        P(("dp", "vol"), None, None),
        P("vol", None, None),
        P("dp", None, None),
        P(),
        P(),
        P(),
        P("dp", None),
        P("dp", None),
        P(),
    )
    return jax.shard_map(
        local,
        mesh=mesh,
        in_specs=placed,
        out_specs=(P(("dp", "vol"), None), P("dp", None), P("dp", None), P()),
        check_vma=False,
    )
```

profile of v0, /device:TPU:0, one launch (start us, length us, event | category | flops | bytes accessed | tf_op | source)
XLA Modules:
  0.0 261.4 jit_solution(18446166115794627641)
XLA Ops:
  8.1 0.7 fusion.38
  8.8 0.7 compare_and_fusion.1
  9.5 11.4 %gather_fusion = bf16[1024,256]{1,0:T(8,128)(2,1)S(1)} fusion(bf16[32768,256]{1,0:T(8,128)(2,1)} %bitcast.106, s32[1024]{0:T(1024)S(1)} %broadcast_clamp_fusion), kind=kCustom, calls=%fused_computation | custom fusion | bytes 1052672 | tf_op jit(solution)/shard_map/jit(_take)/gather | solution.py:67
  21.0 0.2 broadcast_select_fusion
  21.2 10.3 %slice.21 = bf16[1024,128]{1,0:T(8,128)(2,1)S(1)} slice(bf16[1024,256]{1,0:T(8,128)(2,1)S(1)} %broadcast_select_fusion), slice={[0:1024:1], [0:256:2]} | slice | bytes 524288 | tf_op jit(solution)/shard_map/slice | solution.py:67
  31.7 0.8 convert_element_type.102
  32.5 0.5 all-gather.3.cloned.1.call-update
  33.1 0.5 all-gather.5.cloned.1.call-update
  33.6 0.2 reduce-scatter.2.cloned.1.call-start
  33.9 0.5 fusion.21
  34.4 0.5 fusion.19
  35.0 0.6 fusion.24
  35.6 0.6 convert_element_type.105
  36.2 0.3 copy.31
  36.5 0.2 convert_element_type.107
  36.7 0.4 convert_reduce_fusion
  37.2 0.3 fusion.11
  37.5 0.6 dynamic-slice
  38.1 0.6 fusion.9
  38.7 19.9 %all-reduce.9.cloned.1.call-done = bf16[2,65536]{1,0:T(2,128)(2,1)} async-done(((bf16[2,65536]{1,0:T(2,128)(2,1)}), bf16[2,65536]{1,0:T(2,128)(2,1)}) %all-reduce.9.cloned.1.call-update) | async-done | bytes 262160
  58.6 1.8 dynamic-slice_convert_fusion
  60.4 0.6 multiply_reduce_fusion
  61.0 22.6 %all-gather.3.cloned.1.call-done = bf16[1024,1536]{1,0:T(8,128)(2,1)} async-done(((bf16[64,1536]{1,0:T(8,128)(2,1)}), bf16[1024,1536]{1,0:T(8,128)(2,1)}) %all-gather.3.cloned.1.call-update) | async-done | bytes 3145744 | tf_op jit(solution)/shard_map/all_gather | solution.py:99
  83.7 3.0 %convolution_convert_fusion.1 = bf16[256,1536]{1,0:T(8,128)(2,1)S(1)} fusion(bf16[1024,1536]{1,0:T(8,128)(2,1)} %all-gather.3.cloned.1.call-done, bf16[256,1024]{1,0:T(8,128)(2,1)S(1)} %get-tuple-element.9, f32[1024]{0:T(1024)S(1)} %copy-done.17, f32[256]{0:T(256)S(1)} %add_rsqrt_fusion, f32[256]{0:T(256)S(1)} %broadcast_multiply_fusion.2), kind=kOutput, calls=%fused_computation.5 | convolution fusion | flops 807010304 | bytes 4462592 | tf_op jit(solution)/shard_map/dot_general | solution.py:97
  86.7 0.3 copy.32
  87.0 0.5 fusion.63
  87.5 0.3 copy-done.3
  88.0 1.2 convolution_convert_fusion.5
  89.3 32.9 %all-gather.5.cloned.1.call-done = bf16[1024,512]{1,0:T(8,128)(2,1)} async-done(((bf16[64,512]{1,0:T(8,128)(2,1)}), bf16[1024,512]{1,0:T(8,128)(2,1)}) %all-gather.5.cloned.1.call-update) | async-done | bytes 1048592 | tf_op jit(solution)/shard_map/all_gather | solution.py:104
  122.2 1.9 fusion.8
  124.2 0.8 fusion.64
  125.0 1.3 multiply_reduce_fusion.1
  126.3 1.2 subtract_multiply_fusion
  127.7 0.4 copy-done.15
  128.1 1.5 convolution_convert_fusion.3
  129.6 1.1 convolution_convert_fusion.4
  130.7 1.1 copy.34
  131.8 1.5 fusion.4
  133.4 0.6 convolution_bitcast_fusion
  134.0 0.6 convolution_bitcast_fusion.1
  134.6 0.4 convolution_bitcast_fusion.2
  135.1 0.5 copy-done.2
  135.6 1.2 convolution_convert_fusion
  136.8 2.6 pad_maximum_fusion
  139.5 71.4 %reduce-scatter.2.cloned.1.call-done = bf16[64,2048]{1,0:T(8,128)(2,1)} async-done(((bf16[1024,2048]{1,0:T(8,128)(2,1)}), bf16[64,2048]{1,0:T(8,128)(2,1)}) %reduce-scatter.2.cloned.1.call-update) | async-done | bytes 262160 | tf_op jit(solution)/shard_map/reduce_scatter | solution.py:128
  211.0 39.6 %psum.15 = f32[1024,4]{0,1:T(4,128)} all-reduce(f32[1024,4]{0,1:T(4,128)S(1)} %broadcast_multiply_fusion), channel_id=1, replica_groups=mesh['dp'=16,'vol'=2] {'dp','vol'}, use_global_device_ids=true, to_apply=%region_11.12 | all-reduce | flops 4096 | bytes 32768 | tf_op jit(solution)/shard_map/psum | solution.py:113
  250.6 1.7 slice.32
  252.3 1.5 slice.33
  (68 shorter events, 1.1 us)
Async XLA Ops:
  8.0 28.7 %copy-start = (bf16[64,1024]{1,0:T(8,128)(2,1)S(1)}, bf16[64,1024]{1,0:T(8,128)(2,1)}, u32[]{:S(2)}) copy-start(bf16[64,1024]{1,0:T(8,128)(2,1)} %param.14) | copy-start | bytes 393220
  8.0 50.5 %all-reduce.9.cloned.1.call-start = ((), (), s32[]{:S(2)}) async-start(), calls=%async_computation.5 | async-start | bytes 524288
  20.9 13.0 %copy-start.7 = (f32[1,128,128]{2,1,0:T(8,128)S(1)}, f32[1,128,128]{2,1,0:T(8,128)}, u32[]{:S(2)}) copy-start(f32[1,128,128]{2,1,0:T(8,128)} %param.10) | copy-start | bytes 196612
  21.0 14.6 %copy-start.8 = (bf16[1,128,128]{2,1,0:T(8,128)(2,1)S(1)}, bf16[1,128,128]{2,1,0:T(8,128)(2,1)}, u32[]{:S(2)}) copy-start(bf16[1,128,128]{2,1,0:T(8,128)(2,1)} %param.11) | copy-start | bytes 98308
  31.5 5.3 %copy-start.6 = (bf16[256,1024]{1,0:T(8,128)(2,1)S(1)}, bf16[256,1024]{1,0:T(8,128)(2,1)}, u32[]{:S(2)}) copy-start(bf16[256,1024]{1,0:T(8,128)(2,1)} %param.15) | copy-start | bytes 1572868
  32.5 51.2 %all-gather.3.cloned.1.call-start = ((), (), s32[]{:S(2)}) async-start(), calls=%async_computation.1 | async-start | bytes 3342336 | tf_op jit(solution)/shard_map/all_gather | solution.py:99
  33.1 89.2 %all-gather.5.cloned.1.call-start = ((), (), s32[]{:S(2)}) async-start(), calls=%async_computation.2 | async-start | bytes 1114112 | tf_op jit(solution)/shard_map/all_gather | solution.py:104
  33.6 177.2 %reduce-scatter.2.cloned.1.call-start = ((), (), s32[]{:S(2)}) async-start(), calls=%async_computation.3 | async-start | bytes 4456448 | tf_op jit(solution)/shard_map/reduce_scatter | solution.py:128
  34.4 3.1 %copy-start.22 = (u32[32]{0:T(128)S(1)}, u32[32]{0:T(128)}, u32[]{:S(2)}) copy-start(u32[32]{0:T(128)} %constant.104) | copy-start | bytes 388
  36.2 47.5 %copy-start.17 = (f32[1024]{0:T(1024)S(1)}, f32[1024]{0:T(1024)}, u32[]{:S(2)}) copy-start(f32[1024]{0:T(1024)} %param.16) | copy-start | bytes 12292
  37.2 49.5 %copy-start.1 = (bf16[256,1024]{1,0:T(8,128)(2,1)}, bf16[256,1024]{1,0:T(8,128)(2,1)S(1)}, u32[]{:S(2)}) copy-start(bf16[256,1024]{1,0:T(8,128)(2,1)S(1)} %get-tuple-element.9) | copy-start | bytes 1572868
  37.2 49.5 %copy-start.12 = (f32[256]{0:T(256)}, f32[256]{0:T(256)S(1)}, u32[]{:S(2)}) copy-start(f32[256]{0:T(256)S(1)} %broadcast_multiply_fusion.2) | copy-start | bytes 3076
  37.5 49.2 %copy-start.19 = (f32[256]{0:T(256)}, f32[256]{0:T(256)S(1)}, u32[]{:S(2)}) copy-start(f32[256]{0:T(256)S(1)} %add_rsqrt_fusion) | copy-start | bytes 3076
  87.0 0.9 copy-start.3
  122.2 2.0 copy-start.9
  122.2 2.8 %copy-start.14 = (f32[4]{0:T(128)S(1)}, f32[4]{0:T(128)}, u32[]{:S(2)}) copy-start(f32[4]{0:T(128)} %multiply_reduce_fusion) | copy-start | bytes 52
  122.2 7.4 %copy-start.21 = (bf16[1024,512]{1,0:T(8,128)(2,1)S(1)}, bf16[1024,512]{1,0:T(8,128)(2,1)}, u32[]{:S(2)}) copy-start(bf16[1024,512]{1,0:T(8,128)(2,1)} %all-gather.5.cloned.1.call-done) | copy-start | bytes 3145732
  124.2 3.5 %copy-start.10 = (f32[1024]{0:T(1024)}, f32[1024]{0:T(1024)S(1)}, u32[]{:S(2)}) copy-start(f32[1024]{0:T(1024)S(1)} %broadcast_multiply_fusion.1) | copy-start | bytes 12292
  127.5 0.6 copy-start.15
  131.8 1.6 copy-start.4
  134.6 1.0 copy-start.2
  134.6 1.0 copy-start.13
  134.6 1.0 copy-start.18
  134.6 1.0 copy-start.20
  135.6 1.2 copy-start.5
  139.4 71.5 %copy-start.11 = (f32[1024]{0:T(1024)S(1)}, f32[1024]{0:T(1024)}, u32[]{:S(2)}) copy-start(f32[1024]{0:T(1024)} %copy-done.10) | copy-start | bytes 12292
  139.4 71.5 %copy-start.16 = (f32[4]{0:T(128)S(1)}, f32[4]{0:T(128)}, u32[]{:S(2)}) copy-start(f32[4]{0:T(128)} %copy-done.15) | copy-start | bytes 52
  139.4 111.2 %all-reduce.7.cloned.1.call-start = ((), (), s32[]{:S(2)}) async-start(), calls=%async_computation.4 | async-start | bytes 524288 | tf_op jit(solution)/shard_map/psum | solution.py:134
Sparse Core Ops, SparseCore 0:
  32.6 25.9 all-reduce.8
  211.0 22.3 all-reduce.6
Sparse Core Ops, SparseCore 1:
  35.5 48.1 all-gather.2
  85.9 36.2 all-gather.4
  139.5 71.3 reduce-scatter.1
where the time goes:
time: 262 us; the launch traced here: 261 us
  waiting for transfers between devices  148 us (56%)
  blocking collectives  39.6 us (15%)
  local copies, waits for them, and re-layouts  30.1 us (11%)
  matrix products  17.1 us (7%)
  between operations  16.1 us (6%)
  other arithmetic  10.1 us (4%)
    reduce_scatter x1, waiting for transfers between devices, local(): lax.psum_scatter(jnp.concatenate([first, second], axis=1).astype(jnp.bflo...  71.4 us
    psum x1, blocking collectives, local(): lax.psum(jnp.dot(pooled.T, logit_slope, precision=highest), ('dp', 'vol'))  39.6 us
    all_gather x1, waiting for transfers between devices, local(): out_whole = lax.all_gather(project_out, 'dp', axis=0, tiled=True)  32.9 us
    all_gather x1, waiting for transfers between devices, local(): lax.all_gather(project_in, 'dp', axis=0, tiled=True)  22.6 us
    unnamed x6, waiting for transfers between devices  21 us
    gather x1, local copies, waits for them, and re-layouts, render(): picked = jnp.take(table, rows.reshape(-1), axis=0)[:, ::2]  11.4 us
    slice x1, local copies, waits for them, and re-layouts, render(): picked = jnp.take(table, rows.reshape(-1), axis=0)[:, ::2]  10.3 us
  transfers between devices with their start and end apart: 5, of which 4 were waited for; matrix products, arithmetic and copies ran while one was open for 5% of the time, Pallas kernels for 0%

commit v1 on v0

--- a/solution.py
+++ b/solution.py
@@ -110,7 +110,9 @@
     chances = raised / jnp.sum(raised, axis=1, keepdims=True)
     expected = jnp.sum(chances * errors, axis=1, keepdims=True)
     logit_slope = chances * (errors - expected)
-    head_gradient = lax.psum(jnp.dot(pooled.T, logit_slope, precision=highest), ("dp", "vol"))
+    head_gradient = lax.psum(
+        lax.psum(jnp.dot(pooled.T, logit_slope, precision=highest), "vol"), "dp"
+    )
     pooled_slope = jnp.dot(logit_slope, head_weight.T, precision=highest) / PATCHES
     layer_slope = jnp.broadcast_to(pooled_slope[:, None, :], (count, PATCHES, width))
     layer_slope = layer_slope.reshape(count * PATCHES, width).astype(jnp.bfloat16)

time: 262 us -> 288 us (1.099)
  blocking collectives: 39.6 us -> 65.6 us
    psum x1 -> x2, blocking collectives: 39.6 us -> 65.6 us  [the longest x1 57.6 us: local(): lax.psum(lax.psum(jnp.dot(pooled.T, logit_slope, precision=highest), 'vol...]
  transfers between devices with their start and end apart: 5 -> 5, of which waited for: 4 -> 4; matrix products, arithmetic and copies ran while one was open for 5% -> 4% of each run, Pallas kernels for 0% -> 0%
where the time goes in v1:
time: 288 us; the launch traced here: 287 us
  waiting for transfers between devices  148 us (51%)
  blocking collectives  65.6 us (23%)
  local copies, waits for them, and re-layouts  30 us (10%)
  matrix products  17.1 us (6%)
  between operations  16.1 us (6%)
  other arithmetic  10 us (3%)
    reduce_scatter x1, waiting for transfers between devices, local(): lax.psum_scatter(jnp.concatenate([first, second], axis=1).astype(jnp.bflo...  71.4 us
    psum x1, blocking collectives, local(): lax.psum(lax.psum(jnp.dot(pooled.T, logit_slope, precision=highest), 'vol...  57.6 us
    all_gather x1, waiting for transfers between devices, local(): out_whole = lax.all_gather(project_out, 'dp', axis=0, tiled=True)  32.9 us
    all_gather x1, waiting for transfers between devices, local(): lax.all_gather(project_in, 'dp', axis=0, tiled=True)  22.6 us
    unnamed x6, waiting for transfers between devices  21 us
    gather x1, local copies, waits for them, and re-layouts, render(): picked = jnp.take(table, rows.reshape(-1), axis=0)[:, ::2]  11.4 us
    slice x1, local copies, waits for them, and re-layouts, render(): picked = jnp.take(table, rows.reshape(-1), axis=0)[:, ::2]  10.3 us
    psum x1, blocking collectives, local(): lax.psum(jnp.dot(pooled.T, logit_slope, precision=highest), 'vol')  8.01 us
  transfers between devices with their start and end apart: 5, of which 4 were waited for; matrix products, arithmetic and copies ran while one was open for 4% of the time, Pallas kernels for 0%

profile of v1, /device:TPU:0, one launch (start us, length us, event | category | flops | bytes accessed | tf_op | source)
XLA Modules:
  0.0 287.3 jit_solution(14178335303161701951)
XLA Ops:
  8.1 0.7 fusion.38
  8.8 0.7 compare_and_fusion.1
  9.5 11.4 %gather_fusion = bf16[1024,256]{1,0:T(8,128)(2,1)S(1)} fusion(bf16[32768,256]{1,0:T(8,128)(2,1)} %bitcast.106, s32[1024]{0:T(1024)S(1)} %broadcast_clamp_fusion), kind=kCustom, calls=%fused_computation | custom fusion | bytes 1052672 | tf_op jit(solution)/shard_map/jit(_take)/gather | solution.py:67
  21.2 10.3 %slice.21 = bf16[1024,128]{1,0:T(8,128)(2,1)S(1)} slice(bf16[1024,256]{1,0:T(8,128)(2,1)S(1)} %broadcast_select_fusion), slice={[0:1024:1], [0:256:2]} | slice | bytes 524288 | tf_op jit(solution)/shard_map/slice | solution.py:67
  31.7 0.8 convert_element_type.102
  32.5 0.5 all-gather.3.cloned.1.call-update
  33.1 0.5 all-gather.5.cloned.1.call-update
  33.6 0.2 reduce-scatter.2.cloned.1.call-start
  33.9 0.5 fusion.21
  34.4 0.5 fusion.19
  35.0 0.6 fusion.24
  35.6 0.6 convert_element_type.105
  36.2 0.3 copy.31
  36.5 0.2 convert_element_type.107
  36.7 0.4 convert_reduce_fusion
  37.2 0.3 fusion.11
  37.5 0.6 dynamic-slice
  38.1 0.6 fusion.9
  38.7 19.9 %all-reduce.9.cloned.1.call-done = bf16[2,65536]{1,0:T(2,128)(2,1)} async-done(((bf16[2,65536]{1,0:T(2,128)(2,1)}), bf16[2,65536]{1,0:T(2,128)(2,1)}) %all-reduce.9.cloned.1.call-update) | async-done | bytes 262160
  58.6 1.8 dynamic-slice_convert_fusion
  60.4 0.6 multiply_reduce_fusion
  61.0 22.6 %all-gather.3.cloned.1.call-done = bf16[1024,1536]{1,0:T(8,128)(2,1)} async-done(((bf16[64,1536]{1,0:T(8,128)(2,1)}), bf16[1024,1536]{1,0:T(8,128)(2,1)}) %all-gather.3.cloned.1.call-update) | async-done | bytes 3145744 | tf_op jit(solution)/shard_map/all_gather | solution.py:99
  83.7 3.0 %convolution_convert_fusion.1 = bf16[256,1536]{1,0:T(8,128)(2,1)S(1)} fusion(bf16[1024,1536]{1,0:T(8,128)(2,1)} %all-gather.3.cloned.1.call-done, bf16[256,1024]{1,0:T(8,128)(2,1)S(1)} %get-tuple-element.9, f32[1024]{0:T(1024)S(1)} %copy-done.17, f32[256]{0:T(256)S(1)} %add_rsqrt_fusion, f32[256]{0:T(256)S(1)} %broadcast_multiply_fusion.2), kind=kOutput, calls=%fused_computation.5 | convolution fusion | flops 807010304 | bytes 4462592 | tf_op jit(solution)/shard_map/dot_general | solution.py:97
  86.7 0.3 copy.32
  87.0 0.5 fusion.63
  87.5 0.3 copy-done.3
  88.0 1.2 convolution_convert_fusion.5
  89.3 32.9 %all-gather.5.cloned.1.call-done = bf16[1024,512]{1,0:T(8,128)(2,1)} async-done(((bf16[64,512]{1,0:T(8,128)(2,1)}), bf16[1024,512]{1,0:T(8,128)(2,1)}) %all-gather.5.cloned.1.call-update) | async-done | bytes 1048592 | tf_op jit(solution)/shard_map/all_gather | solution.py:104
  122.2 1.9 fusion.8
  124.2 0.8 fusion.64
  125.0 1.3 multiply_reduce_fusion.1
  126.3 1.1 subtract_multiply_fusion
  127.6 0.4 copy-done.15
  128.0 1.5 convolution_convert_fusion.3
  129.4 1.1 convolution_convert_fusion.4
  130.6 1.1 copy.34
  131.7 1.5 fusion.4
  133.2 0.6 convolution_bitcast_fusion
  133.8 0.6 convolution_bitcast_fusion.1
  134.4 0.4 convolution_bitcast_fusion.2
  135.0 0.5 copy-done.2
  135.5 1.2 convolution_convert_fusion
  136.7 2.6 pad_maximum_fusion
  139.3 71.4 %reduce-scatter.2.cloned.1.call-done = bf16[64,2048]{1,0:T(8,128)(2,1)} async-done(((bf16[1024,2048]{1,0:T(8,128)(2,1)}), bf16[64,2048]{1,0:T(8,128)(2,1)}) %reduce-scatter.2.cloned.1.call-update) | async-done | bytes 262160 | tf_op jit(solution)/shard_map/reduce_scatter | solution.py:130
  210.9 8.0 %psum.22 = f32[1024,4]{0,1:T(4,128)S(1)} all-reduce(f32[1024,4]{0,1:T(4,128)S(1)} %broadcast_multiply_fusion), channel_id=1, replica_groups=mesh['dp'=16,'vol'=2] {'vol'}, use_global_device_ids=true, to_apply=%region_11.12 | all-reduce | flops 4096 | bytes 32768 | tf_op jit(solution)/shard_map/psum | solution.py:114
  218.9 57.6 %psum.23 = f32[1024,4]{0,1:T(4,128)} all-reduce(f32[1024,4]{0,1:T(4,128)S(1)} %psum.22), channel_id=1, replica_groups=mesh['dp'=16,'vol'=2] {'dp'}, use_global_device_ids=true, to_apply=%region_12.13 | all-reduce | flops 4096 | bytes 32768 | tf_op jit(solution)/shard_map/psum | solution.py:113
  276.5 1.7 slice.32
  278.2 1.5 slice.33
  (69 shorter events, 1.3 us)
Async XLA Ops:
  8.0 28.7 %copy-start = (bf16[64,1024]{1,0:T(8,128)(2,1)S(1)}, bf16[64,1024]{1,0:T(8,128)(2,1)}, u32[]{:S(2)}) copy-start(bf16[64,1024]{1,0:T(8,128)(2,1)} %param.14) | copy-start | bytes 393220
  8.0 50.5 %all-reduce.9.cloned.1.call-start = ((), (), s32[]{:S(2)}) async-start(), calls=%async_computation.5 | async-start | bytes 524288
  20.9 13.0 %copy-start.7 = (f32[1,128,128]{2,1,0:T(8,128)S(1)}, f32[1,128,128]{2,1,0:T(8,128)}, u32[]{:S(2)}) copy-start(f32[1,128,128]{2,1,0:T(8,128)} %param.10) | copy-start | bytes 196612
  21.0 14.6 %copy-start.8 = (bf16[1,128,128]{2,1,0:T(8,128)(2,1)S(1)}, bf16[1,128,128]{2,1,0:T(8,128)(2,1)}, u32[]{:S(2)}) copy-start(bf16[1,128,128]{2,1,0:T(8,128)(2,1)} %param.11) | copy-start | bytes 98308
  31.5 5.3 %copy-start.6 = (bf16[256,1024]{1,0:T(8,128)(2,1)S(1)}, bf16[256,1024]{1,0:T(8,128)(2,1)}, u32[]{:S(2)}) copy-start(bf16[256,1024]{1,0:T(8,128)(2,1)} %param.15) | copy-start | bytes 1572868
  32.5 51.2 %all-gather.3.cloned.1.call-start = ((), (), s32[]{:S(2)}) async-start(), calls=%async_computation.1 | async-start | bytes 3342336 | tf_op jit(solution)/shard_map/all_gather | solution.py:99
  33.1 89.2 %all-gather.5.cloned.1.call-start = ((), (), s32[]{:S(2)}) async-start(), calls=%async_computation.2 | async-start | bytes 1114112 | tf_op jit(solution)/shard_map/all_gather | solution.py:104
  33.6 177.1 %reduce-scatter.2.cloned.1.call-start = ((), (), s32[]{:S(2)}) async-start(), calls=%async_computation.3 | async-start | bytes 4456448 | tf_op jit(solution)/shard_map/reduce_scatter | solution.py:130
  34.4 3.1 %copy-start.22 = (u32[32]{0:T(128)S(1)}, u32[32]{0:T(128)}, u32[]{:S(2)}) copy-start(u32[32]{0:T(128)} %constant.104) | copy-start | bytes 388
  36.2 47.5 %copy-start.17 = (f32[1024]{0:T(1024)S(1)}, f32[1024]{0:T(1024)}, u32[]{:S(2)}) copy-start(f32[1024]{0:T(1024)} %param.16) | copy-start | bytes 12292
  37.2 49.5 %copy-start.1 = (bf16[256,1024]{1,0:T(8,128)(2,1)}, bf16[256,1024]{1,0:T(8,128)(2,1)S(1)}, u32[]{:S(2)}) copy-start(bf16[256,1024]{1,0:T(8,128)(2,1)S(1)} %get-tuple-element.9) | copy-start | bytes 1572868
  37.2 49.5 %copy-start.12 = (f32[256]{0:T(256)}, f32[256]{0:T(256)S(1)}, u32[]{:S(2)}) copy-start(f32[256]{0:T(256)S(1)} %broadcast_multiply_fusion.2) | copy-start | bytes 3076
  37.5 49.2 %copy-start.19 = (f32[256]{0:T(256)}, f32[256]{0:T(256)S(1)}, u32[]{:S(2)}) copy-start(f32[256]{0:T(256)S(1)} %add_rsqrt_fusion) | copy-start | bytes 3076
  87.0 0.9 copy-start.3
  122.2 2.0 copy-start.9
  122.2 2.8 copy-start.14
  122.2 7.2 %copy-start.21 = (bf16[1024,512]{1,0:T(8,128)(2,1)S(1)}, bf16[1024,512]{1,0:T(8,128)(2,1)}, u32[]{:S(2)}) copy-start(bf16[1024,512]{1,0:T(8,128)(2,1)} %all-gather.5.cloned.1.call-done) | copy-start | bytes 3145732
  124.2 3.4 %copy-start.10 = (f32[1024]{0:T(1024)}, f32[1024]{0:T(1024)S(1)}, u32[]{:S(2)}) copy-start(f32[1024]{0:T(1024)S(1)} %broadcast_multiply_fusion.1) | copy-start | bytes 12292
  127.4 0.5 copy-start.15
  131.7 1.6 copy-start.4
  134.4 1.0 copy-start.2
  134.4 1.0 copy-start.13
  134.4 1.0 copy-start.18
  134.4 1.0 copy-start.20
  135.5 1.2 copy-start.5
  139.3 71.5 %copy-start.11 = (f32[1024]{0:T(1024)S(1)}, f32[1024]{0:T(1024)}, u32[]{:S(2)}) copy-start(f32[1024]{0:T(1024)} %copy-done.10) | copy-start | bytes 12292
  139.3 71.6 %copy-start.16 = (f32[4]{0:T(128)S(1)}, f32[4]{0:T(128)}, u32[]{:S(2)}) copy-start(f32[4]{0:T(128)} %copy-done.15) | copy-start | bytes 52
  139.3 137.2 %all-reduce.7.cloned.1.call-start = ((), (), s32[]{:S(2)}) async-start(), calls=%async_computation.4 | async-start | bytes 524288 | tf_op jit(solution)/shard_map/psum | solution.py:136
Sparse Core Ops, SparseCore 0:
  32.6 25.9 all-reduce.8
  210.9 22.2 all-reduce.6
Sparse Core Ops, SparseCore 1:
  35.5 48.1 all-gather.2
  85.9 36.2 all-gather.4
  139.4 71.4 reduce-scatter.1
